TPU v7x, 32 devices: a whole 2x2x4 slice. The times are simulated.
32 devices in a mesh: band: 2 (over core), grid: 16 (over z, y, x).
Axes of the slice: x: 2, y: 2, z: 4, core: 2. Of those that a mesh axis runs over, the one named last changes fastest.
Arguments:
- coefficients: float32 [4, 2, 128, 128, 128], P('band', None, 'grid'), may hold values from -0.01171875 to 0.01171875
- potential: float32 [128, 128, 128], P('grid'), may hold values from -3 to 3
- external: float32 [128, 128, 128], P('grid'), may hold values from -6 to 6
- core_density: float32 [128, 128, 128], P('grid'), may hold values from 0.05 to 0.5
- rotations: float32 [2, 4, 2], P(None, 'band'), may hold values from -2 to 3
- mlp_in: float32 [3, 32], replicated, may hold values from -4 to 4
- mlp_out: float32 [32], replicated, may hold values from -0.4 to 0.4
Outputs:
- new_coefficients: float32 [4, 2, 128, 128, 128], P('band', None, 'grid')
- new_potential: float32 [128, 128, 128], P('grid')
All inputs are finite; a program needn't handle non-finite values.
Results may differ from a plain program's by a relative error of at most 0.0003.
Values sent between devices are 32-bit elements; how exact they have to be, the bound alone decides.
A program may use at most 64 MiB of HBM per device.

v0:
```python
import math
import jax
import jax.numpy as jnp
from jax import lax
from jax.sharding import PartitionSpec as P

NX = 128
NY = 128
NZ = 128
ITERS = 2
step_size = 0.2
epsilon = 1e-06
spacing = 0.58
kinetic_scale = 0.5 * (2.0 * math.pi / spacing) ** 2
coulomb_scale = spacing * spacing / math.pi
gradient_scale = 2.0 * math.pi / spacing
reduced_scale = 2.0 * (3.0 * math.pi * math.pi) ** (1.0 / 3.0)
exchange_scale = (3.0 / math.pi) ** (1.0 / 3.0)


def frequencies(points, offset, length):
    places = offset + lax.iota(jnp.int32, length)
    return jnp.where(2 * places < points, places, places - points)


def without_nyquist(values, points):
    return jnp.where(2 * values == -points, 0, values)


def reciprocal_tables(offset, length):
    along_x = frequencies(NX, offset, length)
    along_y = frequencies(NY, 0, NY)
    raw_z = frequencies(NZ, 0, NZ)
    along_z = raw_z * (NX // NZ)
    squared = (
        along_x[:, None, None] * along_x[:, None, None]
        + along_y[None, :, None] * along_y[None, :, None]
        + along_z[None, None, :] * along_z[None, None, :]
    )
    cutoff = (16 * squared <= NX * NX).astype(jnp.float32)
    kinetic = kinetic_scale * squared.astype(jnp.float32) / (NX * NX)
    coulomb = jnp.where(
        squared > 0, coulomb_scale * (NX * NX) / jnp.maximum(squared, 1).astype(jnp.float32), 0.0
    )
    slope_x = gradient_scale * without_nyquist(along_x, NX).astype(jnp.float32) / NX
    slope_y = gradient_scale * without_nyquist(along_y, NY).astype(jnp.float32) / NX
    slope_z = gradient_scale * (without_nyquist(raw_z, NZ) * (NX // NZ)).astype(jnp.float32) / NX
    return (
        cutoff,
        kinetic,
        coulomb,
        slope_x[:, None, None],
        slope_y[None, :, None],
        slope_z[None, None, :],
    )


def dft_tables(points, direction):
    places = lax.iota(jnp.int32, points)
    phases = places[:, None] * places[None, :] % points
    angles = phases.astype(jnp.float32) * (2.0 * math.pi / points)
    return (jnp.cos(angles), direction * jnp.sin(angles))


def transform(perceptron_levels, tables, pattern):
    highest = lax.Precision.HIGHEST
    cosine_table, sine_table = tables
    real_part = perceptron_levels[:, 0]
    imag_part = perceptron_levels[:, 1]
    new_real = jnp.einsum(pattern, real_part, cosine_table, precision=highest) - jnp.einsum(
        pattern, imag_part, sine_table, precision=highest
    )
    new_imag = jnp.einsum(pattern, real_part, sine_table, precision=highest) + jnp.einsum(
        pattern, imag_part, cosine_table, precision=highest
    )
    return jnp.stack([new_real, new_imag], 1)


def toward_position_grid(spectral_amplitude, fourier_synthesis, orbital_holder):
    perceptron_levels = transform(spectral_amplitude, fourier_synthesis[2], "bxyz,zw->bxyw")
    perceptron_levels = transform(perceptron_levels, fourier_synthesis[1], "bxyz,yv->bxvz")
    perceptron_levels = orbital_holder(perceptron_levels)
    return transform(perceptron_levels, fourier_synthesis[0], "bxyz,xu->byuz")


def toward_spectral_amplitudes(position_grid_values, fourier_analysis, orbital_holder):
    perceptron_levels = transform(position_grid_values, fourier_analysis[0], "byxz,xu->buyz")
    perceptron_levels = orbital_holder(perceptron_levels)
    perceptron_levels = transform(perceptron_levels, fourier_analysis[1], "bxyz,yv->bxvz")
    perceptron_levels = transform(perceptron_levels, fourier_analysis[2], "bxyz,zw->bxyw")
    return perceptron_levels / (NX * NY * NZ)


def body(coefficients, potential, external, core_density, rotations, mlp_in, mlp_out):
    highest = lax.Precision.HIGHEST
    planes = coefficients.shape[2]
    offset = lax.axis_index("grid") * planes
    cutoff, kinetic, coulomb, slope_x, slope_y, slope_z = reciprocal_tables(offset, planes)
    fourier_synthesis = (dft_tables(NX, 1.0), dft_tables(NY, 1.0), dft_tables(NZ, 1.0))
    fourier_analysis = (dft_tables(NX, -1.0), dft_tables(NY, -1.0), dft_tables(NZ, -1.0))

    def outward(perceptron_levels):
        return lax.all_to_all(perceptron_levels, "grid", split_axis=3, concat_axis=2, tiled=True)

    def inward(perceptron_levels):
        return lax.all_to_all(perceptron_levels, "grid", split_axis=2, concat_axis=3, tiled=True)

    current = cutoff * coefficients
    for iteration in range(ITERS):
        applied = cutoff * (
            kinetic * current
            + toward_spectral_amplitudes(
                toward_position_grid(current, fourier_synthesis, outward) * potential,
                fourier_analysis,
                inward,
            )
        )
        rotation = rotations[iteration]
        intersection, energy = lax.psum(
            (
                jnp.sum(current * current, axis=(1, 2, 3, 4)),
                jnp.sum(current * applied, axis=(1, 2, 3, 4)),
            ),
            "grid",
        )
        factor = 1.0 + step_size * (energy / (intersection + epsilon))
        updated = factor[:, None, None, None, None] * current - step_size * applied
        updated = jnp.einsum("ij,jcxyz->icxyz", rotation, updated, precision=highest)
        length = lax.psum(jnp.sum(updated * updated, axis=(1, 2, 3, 4)), "grid")
        current = updated / jnp.sqrt(length + epsilon)[:, None, None, None, None]
    real_space = toward_position_grid(current, fourier_synthesis, outward)
    bands_all = coefficients.shape[0] * lax.axis_size("band")
    partial_value = 2.0 / bands_all * jnp.sum(real_space * real_space, axis=(0, 1))
    density = lax.psum(partial_value, "band") + core_density
    spectrum = toward_spectral_amplitudes(
        jnp.stack([density, jnp.zeros_like(density)])[None], fourier_analysis, inward
    )[0]
    spec_real = spectrum[0]
    spec_imag = spectrum[1]
    first_real = coulomb * spec_real - slope_x * spec_real
    first_imag = coulomb * spec_imag - slope_x * spec_imag
    second_real = -slope_y * spec_imag - slope_z * spec_real
    second_imag = slope_y * spec_real - slope_z * spec_imag
    fields = toward_position_grid(
        jnp.stack([jnp.stack([first_real, first_imag]), jnp.stack([second_real, second_imag])]),
        fourier_synthesis,
        outward,
    )
    hartree = fields[0, 0]
    change_x = fields[0, 1]
    change_y = fields[1, 0]
    change_z = fields[1, 1]
    cube_root = jnp.cbrt(density)
    gradient = jnp.sqrt(change_x * change_x + change_y * change_y + change_z * change_z)
    reduced = gradient / (reduced_scale * density * cube_root)
    bounded = reduced / (1.0 + reduced)
    hidden = jnp.tanh(
        mlp_in[0][:, None, None, None] * cube_root
        + mlp_in[1][:, None, None, None] * bounded
        + mlp_in[2][:, None, None, None]
    )
    enhance = 1.0 + jnp.einsum("k,kyxz->yxz", mlp_out, hidden, precision=highest)
    new_potential = external + hartree - exchange_scale * cube_root * enhance
    return (current, new_potential)


def solution(mesh):
    in_specs = (
        P("band", None, "grid", None, None),
        P("grid", None, None),
        P("grid", None, None),
        P("grid", None, None),
        P(None, "band", None),
        P(),
        P(),
    )
    out_specs = (P("band", None, "grid", None, None), P("grid", None, None))
    return jax.shard_map(body, mesh=mesh, in_specs=in_specs, out_specs=out_specs, check_vma=False)
```

profile of v0, /device:TPU:12, one launch (start us, length us, event | category | flops | bytes accessed | tf_op | source)
XLA Modules:
  0.0 682.6 jit_solution(3617643584464941430)
XLA Ops:
  21.0 54.6 %all_to_all.126 = f32[2,2,8,128,128]{4,2,0,1,3:T(8,128)S(1)} all-to-all(f32[2,2,8,128,128]{4,2,0,1,3:T(8,128)S(1)} %copy.58), channel_id=1, replica_groups=mesh['band'=2,'grid'=16] {'grid'}, dimensions={3} | all-to-all | bytes 4194304 | tf_op jit(solution)/shard_map/all_to_all | solution.py:103
  86.8 2.5 copy.60
  89.4 16.6 %all-to-all-start.1 = ((f32[2,2,128,8,128]{4,3,0,1,2:T(8,128)}), f32[2,2,128,8,128]{4,3,0,1,2:T(8,128)S(1)}, u32[]{:S(2)}, u32[]{:S(2)}) async-start(f32[2,2,128,8,128]{4,3,0,1,2:T(8,128)} %copy.60), calls=%async_computation.1 | async-start | bytes 4194304 | tf_op jit(solution)/shard_map/all_to_all | solution.py:106
  106.2 46.5 %all-to-all-done.1 = f32[2,2,128,8,128]{4,3,0,1,2:T(8,128)S(1)} async-done(((f32[2,2,128,8,128]{4,3,0,1,2:T(8,128)}), f32[2,2,128,8,128]{4,3,0,1,2:T(8,128)S(1)}, u32[]{:S(2)}, u32[]{:S(2)}) %all-to-all-start.1) | async-done | bytes 2097184 | tf_op jit(solution)/shard_map/all_to_all | solution.py:106
  164.8 29.5 %all-reduce.2 = (f32[2]{0:T(128)S(1)}, f32[2]{0:T(128)S(1)}) all-reduce(f32[2]{0:T(128)S(1)} %get-tuple-element.9, f32[2]{0:T(128)S(1)} %get-tuple-element.8), channel_id=1, replica_groups=mesh['band'=2,'grid'=16] {'grid'}, use_global_device_ids=true, to_apply=%region_1.2 | all-reduce | flops 4 | bytes 32 | tf_op jit(solution)/shard_map/psum | solution.py:119
  194.3 2.3 multiply_subtract_fusion.1
  196.7 9.5 %multiply_reduce_fusion.3 = (f32[2]{0:T(128)S(1)}, f32[2,8,128,128,2]{3,4,2,1,0:T(2,128)S(1)}) fusion(f32[2,2,2]{2,1,0:T(2,128)S(1)} %copy-done.11, f32[2,2,8,128,128]{4,3,2,0,1:T(8,128)S(1)} %multiply_subtract_fusion.1), kind=kOutput, calls=%fused_computation.35 | convolution fusion | flops 13631486 | bytes 4195336 | tf_op jit(solution)/shard_map/ij,jcxyz->icxyz/dot_general | solution.py:128
  206.1 37.0 %psum.51 = f32[2]{0:T(128)S(1)} all-reduce(f32[2]{0:T(128)S(1)} %get-tuple-element.27), channel_id=1, replica_groups=mesh['band'=2,'grid'=16] {'grid'}, use_global_device_ids=true, to_apply=%region_5.6 | all-reduce | flops 2 | bytes 16 | tf_op jit(solution)/shard_map/psum | solution.py:129
  255.1 44.4 %all_to_all.127 = f32[2,2,8,128,128]{4,2,0,1,3:T(8,128)S(1)} all-to-all(f32[2,2,8,128,128]{4,2,0,1,3:T(8,128)S(1)} %copy.72), channel_id=1, replica_groups=mesh['band'=2,'grid'=16] {'grid'}, dimensions={3} | all-to-all | bytes 4194304 | tf_op jit(solution)/shard_map/all_to_all | solution.py:103
  312.0 45.8 %all_to_all.128 = f32[2,2,128,8,128]{4,3,0,1,2:T(8,128)S(1)} all-to-all(f32[2,2,128,8,128]{4,3,0,1,2:T(8,128)S(1)} %copy.74), channel_id=1, replica_groups=mesh['band'=2,'grid'=16] {'grid'}, dimensions={2} | all-to-all | bytes 4194304 | tf_op jit(solution)/shard_map/all_to_all | solution.py:106
  369.3 29.9 %all-reduce.1 = (f32[2]{0:T(128)S(1)}, f32[2]{0:T(128)S(1)}) all-reduce(f32[2]{0:T(128)S(1)} %get-tuple-element.7, f32[2]{0:T(128)S(1)} %get-tuple-element.6), channel_id=1, replica_groups=mesh['band'=2,'grid'=16] {'grid'}, use_global_device_ids=true, to_apply=%region_7.8 | all-reduce | flops 4 | bytes 32 | tf_op jit(solution)/shard_map/psum | solution.py:119
  401.4 9.9 %multiply_reduce_fusion = (f32[2]{0:T(128)S(1)}, f32[2,8,128,128,2]{3,4,2,1,0:T(2,128)}) fusion(f32[2,2,2]{2,1,0:T(2,128)S(1)} %copy-done.11, f32[2,2,8,128,128]{4,3,2,0,1:T(8,128)S(1)} %multiply_subtract_fusion), kind=kOutput, calls=%fused_computation.31 | convolution fusion | flops 13631486 | bytes 4195336 | tf_op jit(solution)/shard_map/ij,jcxyz->icxyz/dot_general | solution.py:128
  411.3 36.7 %psum.54 = f32[2]{0:T(128)S(1)} all-reduce(f32[2]{0:T(128)S(1)} %get-tuple-element.29), channel_id=1, replica_groups=mesh['band'=2,'grid'=16] {'grid'}, use_global_device_ids=true, to_apply=%region_11.12 | all-reduce | flops 2 | bytes 16 | tf_op jit(solution)/shard_map/psum | solution.py:129
  448.0 2.6 divide_bitcast_fusion
  462.6 44.1 %all_to_all.129 = f32[2,2,8,128,128]{4,2,0,1,3:T(8,128)S(1)} all-to-all(f32[2,2,8,128,128]{4,2,0,1,3:T(8,128)S(1)} %copy.89), channel_id=1, replica_groups=mesh['band'=2,'grid'=16] {'grid'}, dimensions={3} | all-to-all | bytes 4194304 | tf_op jit(solution)/shard_map/all_to_all | solution.py:103
  513.2 18.1 %all-reduce.5.cloned.1.call-done = f32[8,128,128]{2,1,0:T(8,128)} async-done(((f32[8,128,128]{2,1,0:T(8,128)}), f32[8,128,128]{2,1,0:T(8,128)}) %all-reduce.5.cloned.1.call-update) | async-done | bytes 524304 | tf_op jit(solution)/shard_map/psum | solution.py:134
  531.3 2.3 fusion.639
  538.7 7.3 %all-to-all-start.5 = ((f32[1,2,128,8,128]{4,3,1,0,2:T(8,128)}), f32[1,2,128,8,128]{4,3,1,0,2:T(8,128)}, u32[]{:S(2)}, u32[]{:S(2)}) async-start(f32[1,2,128,8,128]{4,3,1,0,2:T(8,128)} %copy.91), calls=%async_computation.5 | async-start | bytes 2097152 | tf_op jit(solution)/shard_map/all_to_all | solution.py:106
  546.1 25.3 %all-to-all-done.5 = f32[1,2,128,8,128]{4,3,1,0,2:T(8,128)} async-done(((f32[1,2,128,8,128]{4,3,1,0,2:T(8,128)}), f32[1,2,128,8,128]{4,3,1,0,2:T(8,128)}, u32[]{:S(2)}, u32[]{:S(2)}) %all-to-all-start.5) | async-done | bytes 1048608 | tf_op jit(solution)/shard_map/all_to_all | solution.py:106
  590.8 2.5 copy.101
  593.3 5.9 all-to-all-start.6
  600.9 45.7 %all-to-all-done.6 = f32[2,2,8,128,128]{4,2,0,1,3:T(8,128)} async-done(((f32[2,2,8,128,128]{4,2,0,1,3:T(8,128)}), f32[2,2,8,128,128]{4,2,0,1,3:T(8,128)}, u32[]{:S(2)}, u32[]{:S(2)}) %all-to-all-start.6) | async-done | bytes 2097184 | tf_op jit(solution)/shard_map/all_to_all | solution.py:103
  654.4 4.3 add_tanh_fusion
  658.8 15.2 %fusion = f32[1,8,128,128]{3,0,2,1:T(1,128)S(1)} fusion(f32[32,8,128,128]{3,2,1,0:T(8,128)S(1)} %add_tanh_fusion, f32[32]{0:T(128)S(1)} %copy-done), kind=kOutput, calls=%fused_computation | convolution fusion | flops 50331648 | bytes 17301632 | tf_op jit(solution)/shard_map/k,kyxz->yxz/dot_general | solution.py:162
  (159 shorter events, 128.5 us)
Async XLA Ops:
  7.2 651.6 %copy-start = (f32[32]{0:T(128)S(1)}, f32[32]{0:T(128)}, u32[]{:S(2)}) copy-start(f32[32]{0:T(128)} %param.13) | copy-start | bytes 388
  79.8 1.4 copy-start.6
  89.4 63.3 %all-to-all-start.1 = ((f32[2,2,128,8,128]{4,3,0,1,2:T(8,128)}), f32[2,2,128,8,128]{4,3,0,1,2:T(8,128)S(1)}, u32[]{:S(2)}, u32[]{:S(2)}) async-start(f32[2,2,128,8,128]{4,3,0,1,2:T(8,128)} %copy.60), calls=%async_computation.1 | async-start | bytes 4194304 | tf_op jit(solution)/shard_map/all_to_all | solution.py:106
  106.0 425.3 %all-reduce.5.cloned.1.call-start = ((), (), s32[]{:S(2)}) async-start(), calls=%async_computation.7 | async-start | bytes 1048576 | tf_op jit(solution)/shard_map/psum | solution.py:134
  161.9 2.9 copy-start.4
  161.9 2.0 copy-start.1
  163.9 1.0 copy-start.5
  194.3 2.3 copy-start.11
  303.7 1.4 copy-start.7
  366.9 2.3 copy-start.2
  368.2 1.1 copy-start.3
  512.1 19.1 %copy-start.9 = (f32[8,128,128]{2,1,0:T(8,128)S(1)}, f32[8,128,128]{2,1,0:T(8,128)}, u32[]{:S(2)}) copy-start(f32[8,128,128]{2,1,0:T(8,128)} %param.10) | copy-start | bytes 1572868
  538.7 32.7 %all-to-all-start.5 = ((f32[1,2,128,8,128]{4,3,1,0,2:T(8,128)}), f32[1,2,128,8,128]{4,3,1,0,2:T(8,128)}, u32[]{:S(2)}, u32[]{:S(2)}) async-start(f32[1,2,128,8,128]{4,3,1,0,2:T(8,128)} %copy.91), calls=%async_computation.5 | async-start | bytes 2097152 | tf_op jit(solution)/shard_map/all_to_all | solution.py:106
  593.3 6.0 copy-start.10
  593.3 53.2 %all-to-all-start.6 = ((f32[2,2,8,128,128]{4,2,0,1,3:T(8,128)}), f32[2,2,8,128,128]{4,2,0,1,3:T(8,128)}, u32[]{:S(2)}, u32[]{:S(2)}) async-start(f32[2,2,8,128,128]{4,2,0,1,3:T(8,128)} %copy.101), calls=%async_computation.6 | async-start | bytes 4194304 | tf_op jit(solution)/shard_map/all_to_all | solution.py:103
  658.8 15.3 %copy-start.8 = (f32[8,128,128]{2,1,0:T(8,128)S(1)}, f32[8,128,128]{2,1,0:T(8,128)}, u32[]{:S(2)}) copy-start(f32[8,128,128]{2,1,0:T(8,128)} %param.9) | copy-start | bytes 1572868
Sparse Core Ops, SparseCore 0:
  513.3 17.9 all-reduce.4
where the time goes:
time: 692 us; the launch traced here: 683 us
  blocking collectives  322 us (47%)
  matrix products  137 us (20%)
  waiting for transfers between devices  136 us (20%)
  starting transfers between devices  29.9 us (4%)
  other arithmetic  24 us (3%)
  local copies, waits for them, and re-layouts  18.7 us (3%)
  between operations  15.6 us (2%)
    all_to_all x3, blocking collectives, outward(): lax.all_to_all(perceptron_levels, 'grid', split_axis=3, concat_axis=2, ti...  143 us
    psum x2, blocking collectives, body(): length = lax.psum(jnp.sum(updated * updated, axis=(1, 2, 3, 4)), 'grid')  73.7 us
    all_to_all x2, waiting for transfers between devices, inward(): lax.all_to_all(perceptron_levels, 'grid', split_axis=2, concat_axis=3, ti...  71.8 us
    psum x2, blocking collectives, body(): lax.psum((jnp.sum(current * current, axis=(1, 2, 3, 4)), jnp.sum(current...  59.3 us
    all_to_all x1, blocking collectives, inward(): lax.all_to_all(perceptron_levels, 'grid', split_axis=2, concat_axis=3, ti...  45.8 us
    all_to_all x1, waiting for transfers between devices, outward(): lax.all_to_all(perceptron_levels, 'grid', split_axis=3, concat_axis=2, ti...  45.7 us
    dot_general x21, matrix products, transform(): jnp.einsum(pattern, imag_part, sine_table, precision=highest)  25.9 us
    dot_general x21, matrix products, transform(): jnp.einsum(pattern, imag_part, cosine_table, precision=highest)  25.7 us
  transfers between devices with their start and end apart: 4, of which 4 were waited for; matrix products, arithmetic and copies ran while one was open for 0% of the time, Pallas kernels for 0%

commit v1 on v0

--- a/solution.py
+++ b/solution.py
@@ -16,6 +16,15 @@
 gradient_scale = 2.0 * math.pi / spacing
 reduced_scale = 2.0 * (3.0 * math.pi * math.pi) ** (1.0 / 3.0)
 exchange_scale = (3.0 / math.pi) ** (1.0 / 3.0)
+clear_numbers = lambda shard_axis, array_dim, dim_k, load: jnp.concatenate(
+    lax.all_to_all(
+        jnp.stack(jnp.split(load, lax.axis_size(shard_axis), axis=dim_k)),
+        axis_name=shard_axis,
+        split_axis=0,
+        concat_axis=0,
+    ),
+    axis=array_dim,
+)
 
 
 def frequencies(points, offset, length):
@@ -100,7 +109,7 @@
     fourier_analysis = (dft_tables(NX, -1.0), dft_tables(NY, -1.0), dft_tables(NZ, -1.0))
 
     def outward(perceptron_levels):
-        return lax.all_to_all(perceptron_levels, "grid", split_axis=3, concat_axis=2, tiled=True)
+        return clear_numbers("grid", 2, 3, perceptron_levels)
 
     def inward(perceptron_levels):
         return lax.all_to_all(perceptron_levels, "grid", split_axis=2, concat_axis=3, tiled=True)

time: 692 us -> 687 us (level)
  starting transfers between devices: 29.9 us -> 18.5 us
  other arithmetic: 24 us -> 34.8 us
    all_to_all x2, starting transfers between devices: 23.9 us -> 12.8 us  [inward(): lax.all_to_all(perceptron_levels, 'grid', split_axis=2, concat_axis=3, ti...]
    unnamed x0 -> x60, other arithmetic: none -> 10.9 us
where the time goes in v1:
time: 687 us; the launch traced here: 678 us
  blocking collectives  323 us (47%)
  matrix products  137 us (20%)
  waiting for transfers between devices  137 us (20%)
  other arithmetic  34.8 us (5%)
  starting transfers between devices  18.5 us (3%)
  between operations  15.7 us (2%)
  local copies, waits for them, and re-layouts  12.8 us (2%)
    all_to_all x3, blocking collectives, lax.all_to_all(jnp.stack(jnp.split(load, lax.axis_size(shard_axis), axis=...  144 us
    psum x2, blocking collectives, body(): length = lax.psum(jnp.sum(updated * updated, axis=(1, 2, 3, 4)), 'grid')  73.1 us
    all_to_all x2, waiting for transfers between devices, inward(): lax.all_to_all(perceptron_levels, 'grid', split_axis=2, concat_axis=3, ti...  72.7 us
    psum x2, blocking collectives, body(): lax.psum((jnp.sum(current * current, axis=(1, 2, 3, 4)), jnp.sum(current...  59.4 us
    all_to_all x1, blocking collectives, inward(): lax.all_to_all(perceptron_levels, 'grid', split_axis=2, concat_axis=3, ti...  46 us
    all_to_all x1, waiting for transfers between devices, lax.all_to_all(jnp.stack(jnp.split(load, lax.axis_size(shard_axis), axis=...  45.9 us
    dot_general x21, matrix products, transform(): jnp.einsum(pattern, imag_part, sine_table, precision=highest)  25.8 us
    dot_general x21, matrix products, transform(): jnp.einsum(pattern, imag_part, cosine_table, precision=highest)  25.7 us
  transfers between devices with their start and end apart: 4, of which 4 were waited for; matrix products, arithmetic and copies ran while one was open for 0% of the time, Pallas kernels for 0%

profile of v1, /device:TPU:12, one launch (start us, length us, event | category | flops | bytes accessed | tf_op | source)
XLA Modules:
  0.0 678.4 jit_solution(9342625213865868539)
XLA Ops:
  19.9 54.8 %all_to_all.74 = f32[16,2,2,8,8,128]{5,4,3,1,2,0:T(8,128)S(1)} all-to-all(f32[16,2,2,8,8,128]{5,4,3,1,2,0:T(8,128)S(1)} %constant_dynamic-update-slice_fusion), channel_id=1, replica_groups=mesh['band'=2,'grid'=16] {'grid'}, dimensions={0} | all-to-all | bytes 4194304 | tf_op jit(solution)/shard_map/all_to_all | solution.py:20
  86.2 2.5 copy.109
  88.7 5.5 all-to-all-start.1
  94.5 47.4 %all-to-all-done.1 = f32[2,2,128,8,128]{4,3,0,1,2:T(8,128)S(1)} async-done(((f32[2,2,128,8,128]{4,3,0,1,2:T(8,128)}), f32[2,2,128,8,128]{4,3,0,1,2:T(8,128)S(1)}, u32[]{:S(2)}, u32[]{:S(2)}) %all-to-all-start.1) | async-done | bytes 2097184 | tf_op jit(solution)/shard_map/all_to_all | solution.py:115
  154.0 29.7 %all-reduce.2 = (f32[2]{0:T(128)S(1)}, f32[2]{0:T(128)S(1)}) all-reduce(f32[2]{0:T(128)S(1)} %get-tuple-element.11, f32[2]{0:T(128)S(1)} %get-tuple-element.10), channel_id=1, replica_groups=mesh['band'=2,'grid'=16] {'grid'}, use_global_device_ids=true, to_apply=%region_1.2 | all-reduce | flops 4 | bytes 32 | tf_op jit(solution)/shard_map/psum | solution.py:128
  183.8 2.3 multiply_subtract_fusion.1
  186.1 9.5 %multiply_reduce_fusion.3 = (f32[2]{0:T(128)S(1)}, f32[2,8,128,128,2]{3,4,2,1,0:T(2,128)S(1)}) fusion(f32[2,2,2]{2,1,0:T(2,128)S(1)} %copy-done.11, f32[2,2,8,128,128]{4,3,2,0,1:T(8,128)S(1)} %multiply_subtract_fusion.1), kind=kOutput, calls=%fused_computation.147 | convolution fusion | flops 13631486 | bytes 4195336 | tf_op jit(solution)/shard_map/ij,jcxyz->icxyz/dot_general | solution.py:137
  195.5 36.2 %psum.51 = f32[2]{0:T(128)S(1)} all-reduce(f32[2]{0:T(128)S(1)} %get-tuple-element.37), channel_id=1, replica_groups=mesh['band'=2,'grid'=16] {'grid'}, use_global_device_ids=true, to_apply=%region_5.6 | all-reduce | flops 2 | bytes 16 | tf_op jit(solution)/shard_map/psum | solution.py:138
  242.7 45.2 %all_to_all.75 = f32[16,2,2,8,8,128]{5,4,3,1,2,0:T(8,128)S(1)} all-to-all(f32[16,2,2,8,8,128]{5,4,3,1,2,0:T(8,128)S(1)} %constant_dynamic-update-slice_fusion.16), channel_id=1, replica_groups=mesh['band'=2,'grid'=16] {'grid'}, dimensions={0} | all-to-all | bytes 4194304 | tf_op jit(solution)/shard_map/all_to_all | solution.py:20
  300.5 46.0 %all_to_all.76 = f32[2,2,128,8,128]{4,3,0,1,2:T(8,128)S(1)} all-to-all(f32[2,2,128,8,128]{4,3,0,1,2:T(8,128)S(1)} %copy.124), channel_id=1, replica_groups=mesh['band'=2,'grid'=16] {'grid'}, dimensions={2} | all-to-all | bytes 4194304 | tf_op jit(solution)/shard_map/all_to_all | solution.py:115
  358.0 29.7 %all-reduce.1 = (f32[2]{0:T(128)S(1)}, f32[2]{0:T(128)S(1)}) all-reduce(f32[2]{0:T(128)S(1)} %get-tuple-element.9, f32[2]{0:T(128)S(1)} %get-tuple-element.8), channel_id=1, replica_groups=mesh['band'=2,'grid'=16] {'grid'}, use_global_device_ids=true, to_apply=%region_7.8 | all-reduce | flops 4 | bytes 32 | tf_op jit(solution)/shard_map/psum | solution.py:128
  387.8 2.3 multiply_subtract_fusion
  390.0 9.9 %multiply_reduce_fusion = (f32[2]{0:T(128)S(1)}, f32[2,8,128,128,2]{3,4,2,1,0:T(2,128)}) fusion(f32[2,2,2]{2,1,0:T(2,128)S(1)} %copy-done.11, f32[2,2,8,128,128]{4,3,2,0,1:T(8,128)S(1)} %multiply_subtract_fusion), kind=kOutput, calls=%fused_computation.143 | convolution fusion | flops 13631486 | bytes 4195336 | tf_op jit(solution)/shard_map/ij,jcxyz->icxyz/dot_general | solution.py:137
  399.9 37.0 %psum.54 = f32[2]{0:T(128)S(1)} all-reduce(f32[2]{0:T(128)S(1)} %get-tuple-element.39), channel_id=1, replica_groups=mesh['band'=2,'grid'=16] {'grid'}, use_global_device_ids=true, to_apply=%region_11.12 | all-reduce | flops 2 | bytes 16 | tf_op jit(solution)/shard_map/psum | solution.py:138
  436.9 2.6 divide_bitcast_fusion
  450.2 44.5 %all_to_all.77 = f32[16,2,2,8,8,128]{5,4,3,1,2,0:T(8,128)S(1)} all-to-all(f32[16,2,2,8,8,128]{5,4,3,1,2,0:T(8,128)S(1)} %constant_dynamic-update-slice_fusion.32), channel_id=1, replica_groups=mesh['band'=2,'grid'=16] {'grid'}, dimensions={0} | all-to-all | bytes 4194304 | tf_op jit(solution)/shard_map/all_to_all | solution.py:20
  501.4 18.1 %all-reduce.5.cloned.1.call-done = f32[8,128,128]{2,1,0:T(8,128)} async-done(((f32[8,128,128]{2,1,0:T(8,128)}), f32[8,128,128]{2,1,0:T(8,128)}) %all-reduce.5.cloned.1.call-update) | async-done | bytes 524304 | tf_op jit(solution)/shard_map/psum | solution.py:143
  519.4 2.3 fusion.703
  526.9 7.3 %all-to-all-start.5 = ((f32[1,2,128,8,128]{4,3,1,0,2:T(8,128)}), f32[1,2,128,8,128]{4,3,1,0,2:T(8,128)}, u32[]{:S(2)}, u32[]{:S(2)}) async-start(f32[1,2,128,8,128]{4,3,1,0,2:T(8,128)} %copy.142), calls=%async_computation.5 | async-start | bytes 2097152 | tf_op jit(solution)/shard_map/all_to_all | solution.py:115
  534.3 25.3 %all-to-all-done.5 = f32[1,2,128,8,128]{4,3,1,0,2:T(8,128)} async-done(((f32[1,2,128,8,128]{4,3,1,0,2:T(8,128)}), f32[1,2,128,8,128]{4,3,1,0,2:T(8,128)}, u32[]{:S(2)}, u32[]{:S(2)}) %all-to-all-start.5) | async-done | bytes 1048608 | tf_op jit(solution)/shard_map/all_to_all | solution.py:115
  589.4 5.6 all-to-all-start.6
  596.7 45.9 %all-to-all-done.6 = f32[16,2,2,8,8,128]{5,4,3,1,2,0:T(8,128)} async-done(((f32[16,2,2,8,8,128]{5,4,3,1,2,0:T(8,128)}), f32[16,2,2,8,8,128]{5,4,3,1,2,0:T(8,128)}, u32[]{:S(2)}, u32[]{:S(2)}) %all-to-all-start.6) | async-done | bytes 2097184 | tf_op jit(solution)/shard_map/all_to_all | solution.py:20
  650.5 4.3 add_tanh_fusion
  654.9 15.2 %fusion = f32[1,8,128,128]{3,0,2,1:T(1,128)S(1)} fusion(f32[32,8,128,128]{3,2,1,0:T(8,128)S(1)} %add_tanh_fusion, f32[32]{0:T(128)S(1)} %copy-done), kind=kOutput, calls=%fused_computation | convolution fusion | flops 50331648 | bytes 17301632 | tf_op jit(solution)/shard_map/k,kyxz->yxz/dot_general | solution.py:171
  (219 shorter events, 133.8 us)
Async XLA Ops:
  7.2 647.7 %copy-start = (f32[32]{0:T(128)S(1)}, f32[32]{0:T(128)}, u32[]{:S(2)}) copy-start(f32[32]{0:T(128)} %param.13) | copy-start | bytes 388
  79.1 1.4 copy-start.6
  88.7 53.2 %all-to-all-start.1 = ((f32[2,2,128,8,128]{4,3,0,1,2:T(8,128)}), f32[2,2,128,8,128]{4,3,0,1,2:T(8,128)S(1)}, u32[]{:S(2)}, u32[]{:S(2)}) async-start(f32[2,2,128,8,128]{4,3,0,1,2:T(8,128)} %copy.109), calls=%async_computation.1 | async-start | bytes 4194304 | tf_op jit(solution)/shard_map/all_to_all | solution.py:115
  94.2 425.2 %all-reduce.5.cloned.1.call-start = ((), (), s32[]{:S(2)}) async-start(), calls=%async_computation.7 | async-start | bytes 1048576 | tf_op jit(solution)/shard_map/psum | solution.py:143
  151.0 2.9 copy-start.4
  151.1 2.0 copy-start.1
  153.0 1.0 copy-start.5
  183.8 2.3 copy-start.11
  292.2 1.4 copy-start.7
  355.7 2.3 copy-start.2
  357.0 1.1 copy-start.3
  500.3 19.1 %copy-start.9 = (f32[8,128,128]{2,1,0:T(8,128)S(1)}, f32[8,128,128]{2,1,0:T(8,128)}, u32[]{:S(2)}) copy-start(f32[8,128,128]{2,1,0:T(8,128)} %param.10) | copy-start | bytes 1572868
  526.9 32.7 %all-to-all-start.5 = ((f32[1,2,128,8,128]{4,3,1,0,2:T(8,128)}), f32[1,2,128,8,128]{4,3,1,0,2:T(8,128)}, u32[]{:S(2)}, u32[]{:S(2)}) async-start(f32[1,2,128,8,128]{4,3,1,0,2:T(8,128)} %copy.142), calls=%async_computation.5 | async-start | bytes 2097152 | tf_op jit(solution)/shard_map/all_to_all | solution.py:115
  589.4 5.6 copy-start.10
  589.4 53.1 %all-to-all-start.6 = ((f32[16,2,2,8,8,128]{5,4,3,1,2,0:T(8,128)}), f32[16,2,2,8,8,128]{5,4,3,1,2,0:T(8,128)}, u32[]{:S(2)}, u32[]{:S(2)}) async-start(f32[16,2,2,8,8,128]{5,4,3,1,2,0:T(8,128)} %constant_dynamic-update-slice_fusion.48), calls=%async_computation.6 | async-start | bytes 4194304 | tf_op jit(solution)/shard_map/all_to_all | solution.py:20
  654.8 15.2 %copy-start.8 = (f32[8,128,128]{2,1,0:T(8,128)S(1)}, f32[8,128,128]{2,1,0:T(8,128)}, u32[]{:S(2)}) copy-start(f32[8,128,128]{2,1,0:T(8,128)} %param.9) | copy-start | bytes 1572868
Sparse Core Ops, SparseCore 0:
  501.5 17.8 all-reduce.4
